TPU v7x, 256 devices: a whole 4x4x8 slice. The times are simulated.
256 devices in a mesh: dp: 8 (over y, core), expert: 32 (over x, z).
Axes of the slice: x: 4, y: 4, z: 8, core: 2. Of those that a mesh axis runs over, the one named last changes fastest.
Arguments:
- tokens: bfloat16 [8192, 3584], P('expert', 'dp'), may hold values from -6 to 6
- cotangent: bfloat16 [8192, 3584], P('expert', 'dp'), may hold values from -6 to 6
- slot_tokens: int32 [32, 32, 32], P('expert'), may hold values from 0 to 255
- slot_counts: int32 [32, 32], P('expert'), may hold values from 0 to 32, as said below
- slot_gates: float32 [32, 32, 32], P('expert'), may hold values from 0.1 to 1
- swap_pairs: int32 [16], replicated, may hold values from 0 to 1, as said below
- gate_weight: bfloat16 [32, 3584, 1024], P('expert', 'dp'), may hold values from -0.09375 to 0.09375
- up_weight: bfloat16 [32, 3584, 1024], P('expert', 'dp'), may hold values from -0.09375 to 0.09375
- down_weight: bfloat16 [32, 1024, 3584], P('expert', None, 'dp'), may hold values from -0.1875 to 0.1875
- first_moment: float32 [32, 1024, 3584], P('expert', None, 'dp'), may hold values from -6 to 6
- second_moment: float32 [32, 1024, 3584], P('expert', None, 'dp'), may hold values from 0.5 to 4
Outputs:
- mixed: bfloat16 [8192, 3584], P('expert', 'dp')
- token_grad: bfloat16 [8192, 3584], P('expert', 'dp')
- new_first_moment: float32 [32, 1024, 3584], P('expert', None, 'dp')
- new_second_moment: float32 [32, 1024, 3584], P('expert', None, 'dp')
- adam_step: bfloat16 [32, 1024, 3584], P('expert', None, 'dp')
Inputs may be any that keep to these rules, and one draw needn't show every extreme that they name: `slot_tokens`: slots at or past slot_counts hold arbitrary token numbers and carry nothing. `slot_counts`: every source fills all 32 slots of some expert, and one expert receives 32 live slots from every source. `swap_pairs`: at least one pair trades and at least one pair does not.
All inputs are finite; a program needn't handle non-finite values.
Results may differ from a plain program's by a relative error of at most 0.022.
Values may be sent and summed in bfloat16 or wider, within the bound.
No kernel may reach another device: no remote copies, remote signals or barrier semaphores. Data moves between devices by JAX's collectives and lax.ppermute only.
A program may use at most 128 MiB of HBM per device.

v0:
```python
import jax
import jax.numpy as jnp
from jax import lax
from jax.sharding import PartitionSpec as P

beta_first = 0.9
beta_second = 0.999
adam_eps = 1e-08


def partner(block, axis, bit):
    count = lax.axis_size(axis)
    route = []
    for low in range(count):
        high = low | 1 << bit
        if high != low and high < count:
            route += [(low, high), (high, low)]
    return lax.ppermute(block, axis, route)


def held_order(values, pair_flags):
    half_count = pair_flags.shape[0]
    blocks = values.reshape((2, half_count) + values.shape[1:])
    chosen = pair_flags.reshape((1, half_count) + (1,) * (values.ndim - 1)) > 0
    return jnp.where(chosen, blocks[::-1], blocks).reshape(values.shape)


def preact_grad(hidden_grad, gate_pre, up_pre):
    sigmoid_gate = jax.nn.sigmoid(gate_pre)
    first_half = hidden_grad * up_pre * sigmoid_gate * (1.0 + gate_pre * (1.0 - sigmoid_gate))
    second_half = hidden_grad * gate_pre * sigmoid_gate
    return jnp.concatenate([first_half, second_half], axis=1).astype(jnp.bfloat16)


def shards(
    tokens,
    cotangent,
    slot_tokens,
    slot_counts,
    slot_gates,
    swap_pairs,
    gate_weight,
    up_weight,
    down_weight,
    first_moment,
    second_moment,
):
    tok_count, model_cols = tokens.shape
    experts = slot_counts.shape[1]
    capacity = slot_tokens.shape[2]
    bit_index = lax.axis_size("expert").bit_length() - 2
    position = lax.axis_index("expert")
    half_count = swap_pairs.shape[0]
    own_swap = (
        jnp.sum(jnp.where(jnp.arange(half_count) == position % half_count, swap_pairs, 0)) > 0
    )
    live_slots = (
        (jnp.arange(capacity)[None, :] < slot_counts[0][:, None]).astype(jnp.float32).reshape(-1)
    )
    weighted = live_slots * slot_gates[0].reshape(-1)
    slot_route = slot_tokens[0].reshape(-1)
    matcher = (jnp.arange(tok_count)[:, None] == slot_route[None, :]).astype(jnp.float32)
    gate_up = jnp.concatenate([gate_weight[0], up_weight[0]], axis=1)
    down_proj = down_weight[0]
    moment_one = first_moment[0]
    moment_two = second_moment[0]
    moved_gate_up, moved_down = partner((gate_up, down_proj), "expert", bit_index)
    gate_up = jnp.where(own_swap, moved_gate_up, gate_up)
    down_proj = jnp.where(own_swap, moved_down, down_proj)
    moved_one, moved_two = (
        partner(moment_one.astype(jnp.bfloat16), "expert", bit_index).astype(moment_one.dtype),
        partner(moment_two.astype(jnp.bfloat16), "expert", bit_index).astype(moment_two.dtype),
    )
    moment_one = jnp.where(own_swap, moved_one, moment_one)
    moment_two = jnp.where(own_swap, moved_two, moment_two)

    def to_hosts(slot_rows):
        return held_order(slot_rows, swap_pairs)

    picked = jnp.take(tokens, slot_route, axis=0)
    outgoing = jnp.where(live_slots[:, None] > 0, picked, jnp.zeros_like(picked)).reshape(
        experts, capacity, model_cols
    )
    arrived = lax.all_to_all(
        to_hosts(outgoing), "expert", split_axis=0, concat_axis=0, tiled=True
    ).reshape(-1, model_cols)
    hidden_units = down_proj.shape[0]
    contract_last = (((1,), (1,)), ((), ()))
    preact = lax.psum(
        jnp.dot(arrived, gate_up, preferred_element_type=jnp.float32).astype(jnp.bfloat16), "dp"
    ).astype(jnp.float32)
    gate_pre = preact[:, :hidden_units]
    up_pre = preact[:, hidden_units:]
    hidden = (jax.nn.silu(gate_pre) * up_pre).astype(jnp.bfloat16)
    outputs = (
        jnp.dot(hidden, down_proj, preferred_element_type=jnp.float32)
        .astype(jnp.bfloat16)
        .reshape(-1, capacity, model_cols)
    )
    returned = to_hosts(
        lax.all_to_all(outputs, "expert", split_axis=0, concat_axis=0, tiled=True)
    ).reshape(-1, model_cols)
    mixed = jnp.dot(
        matcher * weighted[None, :], returned.astype(jnp.float32), precision=lax.Precision.HIGHEST
    ).astype(jnp.bfloat16)
    grad_picked = jnp.take(cotangent, slot_route, axis=0).astype(jnp.float32) * weighted[:, None]
    grad_slots = grad_picked.astype(jnp.bfloat16).reshape(experts, capacity, model_cols)
    arrived_grad = lax.all_to_all(
        to_hosts(grad_slots), "expert", split_axis=0, concat_axis=0, tiled=True
    ).reshape(-1, model_cols)
    weight_grad = lax.dot_general(
        hidden, arrived_grad, (((0,), (0,)), ((), ())), preferred_element_type=jnp.float32
    )
    hidden_grad = lax.psum(
        lax.dot_general(
            arrived_grad, down_proj, contract_last, preferred_element_type=jnp.float32
        ).astype(jnp.bfloat16),
        "dp",
    ).astype(jnp.float32)
    back_rows = lax.dot_general(
        preact_grad(hidden_grad, gate_pre, up_pre),
        gate_up,
        contract_last,
        preferred_element_type=jnp.float32,
    ).astype(jnp.bfloat16)
    returned_grad = to_hosts(
        lax.all_to_all(
            back_rows.reshape(-1, capacity, model_cols),
            "expert",
            split_axis=0,
            concat_axis=0,
            tiled=True,
        )
    ).reshape(-1, model_cols)
    token_grad = jnp.dot(
        matcher * live_slots[None, :],
        returned_grad.astype(jnp.float32),
        precision=lax.Precision.HIGHEST,
    ).astype(jnp.bfloat16)
    new_one = beta_first * moment_one + (1.0 - beta_first) * weight_grad
    new_two = beta_second * moment_two + (1.0 - beta_second) * weight_grad * weight_grad
    step_dir = (new_one / (jnp.sqrt(new_two) + adam_eps)).astype(jnp.bfloat16)
    return (mixed, token_grad, new_one[None], new_two[None], step_dir[None])


def solution(mesh):
    return jax.shard_map(
        shards,
        mesh=mesh,
        in_specs=(
            P("expert", "dp"),
            P("expert", "dp"),
            P("expert", None, None),
            P("expert", None),
            P("expert", None, None),
            P(),
            P("expert", "dp", None),
            P("expert", "dp", None),
            P("expert", None, "dp"),
            P("expert", None, "dp"),
            P("expert", None, "dp"),
        ),
        out_specs=(
            P("expert", "dp"),
            P("expert", "dp"),
            P("expert", None, "dp"),
            P("expert", None, "dp"),
            P("expert", None, "dp"),
        ),
        check_vma=False,
    )
```

profile of v0, /device:TPU:1, one launch (start us, length us, event | category | flops | bytes accessed | tf_op | source)
XLA Modules:
  0.0 329.5 jit_solution(159144839303572518)
XLA Ops:
  11.0 4.0 %gather_fusion = bf16[1024,448]{1,0:T(8,128)(2,1)S(1)} fusion(bf16[256,448]{1,0:T(8,128)(2,1)S(1)} %copy.22, s32[1024]{0:T(1024)S(1)} %fusion.26), kind=kCustom, calls=%fused_computation.clone | custom fusion | bytes 1839104 | tf_op jit(solution)/shard_map/jit(_take)/gather | solution.py:80
  15.0 4.0 %gather_fusion.1 = bf16[1024,448]{1,0:T(8,128)(2,1)S(1)} fusion(bf16[256,448]{1,0:T(8,128)(2,1)S(1)} %copy.24, s32[1024]{0:T(1024)S(1)} %fusion.26), kind=kCustom, calls=%fused_computation.1.clone | custom fusion | bytes 1839104 | tf_op jit(solution)/shard_map/jit(_take)/gather | solution.py:106
  20.2 2.2 reverse_select_fusion.1
  22.4 11.9 %all-to-all-start.2 = ((bf16[32,32,448]{2,1,0:T(8,128)(2,1)}), bf16[32,32,448]{2,1,0:T(8,128)(2,1)S(1)}, u32[]{:S(2)}, u32[]{:S(2)}) async-start(bf16[32,32,448]{2,1,0:T(8,128)(2,1)} %bitcast.11), calls=%async_computation.2 | async-start | bytes 2097152 | tf_op jit(solution)/shard_map/all_to_all | solution.py:108
  35.8 2.8 collective-permute-start
  38.6 20.5 %all-to-all-done.2 = bf16[32,32,448]{2,1,0:T(8,128)(2,1)S(1)} async-done(((bf16[32,32,448]{2,1,0:T(8,128)(2,1)}), bf16[32,32,448]{2,1,0:T(8,128)(2,1)S(1)}, u32[]{:S(2)}, u32[]{:S(2)}) %all-to-all-start.2) | async-done | bytes 917536 | tf_op jit(solution)/shard_map/all_to_all | solution.py:108
  59.1 8.4 %all-to-all-start = ((bf16[32,32,448]{2,1,0:T(8,128)(2,1)}), bf16[32,32,448]{2,1,0:T(8,128)(2,1)}, u32[]{:S(2)}, u32[]{:S(2)}) async-start(bf16[32,32,448]{2,1,0:T(8,128)(2,1)} %bitcast.2), calls=%async_computation | async-start | bytes 2097152 | tf_op jit(solution)/shard_map/all_to_all | solution.py:84
  67.6 2.8 collective-permute-start.1
  71.6 48.7 %collective-permute-done.1 = bf16[1024,448]{0,1:T(8,128)(2,1)} collective-permute-done((bf16[1024,448]{0,1:T(8,128)(2,1)}, bf16[1024,448]{0,1:T(8,128)(2,1)}, u32[]{:S(2)}, u32[]{:S(2)}) %collective-permute-start.1) | collective-permute-done | bytes 917536 | tf_op jit(solution)/shard_map/ppermute | solution.py:18
  120.3 3.8 %convolution_convert_fusion.1 = bf16[1024,1024]{1,0:T(8,128)(2,1)} fusion(bf16[1024,448]{1,0:T(8,128)(2,1)S(1)} %bitcast.65, bf16[1024,448]{0,1:T(8,128)(2,1)} %collective-permute-done.1, pred[]{:T(512)S(6)} %gt.21, bf16[1,1024,448]{1,2,0:T(8,128)(2,1)} %param.21), kind=kOutput, calls=%fused_computation.18 | convolution fusion | flops 941031424 | bytes 4849665 | tf_op jit(solution)/shard_map/dot_general | solution.py:115
  124.2 6.1 %convolution_convert_fusion = bf16[1024,2048]{1,0:T(8,128)(2,1)} fusion(bf16[1024,448]{1,0:T(8,128)(2,1)} %bitcast.3, bf16[448,2048]{1,0:T(8,128)(2,1)} %collective-permute-done, pred[]{:T(512)S(6)} %gt.21, bf16[448,1024]{1,0:T(8,128)(2,1)} %bitcast.68, bf16[448,1024]{1,0:T(8,128)(2,1)} %bitcast.71), kind=kOutput, calls=%fused_computation.15 | convolution fusion | flops 1885732864 | bytes 8781825 | tf_op jit(solution)/shard_map/dot_general | solution.py:90
  130.3 90.2 %all-reduce.3.cloned.1.call-done = (bf16[1024,2048]{1,0:T(8,128)(2,1)}, bf16[1024,1024]{1,0:T(8,128)(2,1)}) async-done(((bf16[1024,2048]{1,0:T(8,128)(2,1)}, bf16[1024,1024]{1,0:T(8,128)(2,1)}), (bf16[1024,2048]{1,0:T(8,128)(2,1)}, bf16[1024,1024]{1,0:T(8,128)(2,1)})) %all-reduce.3.cloned.1.call-update) | async-done | bytes 6291472 | tf_op jit(solution)/shard_map/psum | solution.py:89
  220.5 3.4 %convert_element_type.69 = f32[1024,2048]{1,0:T(8,128)S(1)} convert(bf16[1024,2048]{1,0:T(8,128)(2,1)} %get-tuple-element.6) | non-fusion elementwise | flops 2097152 | bytes 12582912 | tf_op jit(solution)/shard_map/convert_element_type | solution.py:91
  224.0 3.7 %fusion.2 = (bf16[1024,1024]{1,0:T(8,128)(2,1)S(1)}, bf16[1024,1024]{1,0:T(8,128)(2,1)}, bf16[1024,1024]{1,0:T(8,128)(2,1)S(1)}) fusion(bf16[1024,1024]{1,0:T(8,128)(2,1)S(1)} %copy-done.3, f32[1024,2048]{1,0:T(8,128)S(1)} %convert_element_type.69), kind=kLoop, calls=%fused_computation.6 | loop fusion | flops 17825792 | bytes 16777216 | tf_op jit(solution)/shard_map/convert
  231.4 10.7 %all-to-all-start.1 = ((bf16[32,32,448]{2,1,0:T(8,128)(2,1)}), bf16[32,32,448]{2,1,0:T(8,128)(2,1)S(1)}, u32[]{:S(2)}, u32[]{:S(2)}) async-start(bf16[32,32,448]{2,1,0:T(8,128)(2,1)} %bitcast.7), calls=%async_computation.1 | async-start | bytes 2097152 | tf_op jit(solution)/shard_map/all_to_all | solution.py:101
  242.2 2.7 bitcast_convert_fusion.1
  244.9 2.7 collective-permute-start.2
  247.6 4.6 %fusion.13 = bf16[1024,448]{0,1:T(8,128)(2,1)} fusion(bf16[1024,1024]{1,0:T(8,128)(2,1)S(1)} %copy-done.2, bf16[1024,1024]{1,0:T(8,128)(2,1)S(1)} %get-tuple-element.8, bf16[448,2048]{1,0:T(8,128)(2,1)} %collective-permute-done, pred[]{:T(512)S(6)} %gt.21, bf16[448,1024]{1,0:T(8,128)(2,1)} %bitcast.69, bf16[448,1024]{1,0:T(8,128)(2,1)} %bitcast.72), kind=kOutput, calls=%fused_computation.34 | convolution fusion | flops 1892483072 | bytes 8781825 | tf_op jit(solution)/shard_map/dot_general | solution.py:120
  252.3 2.2 copy.25
  254.5 12.8 %all-to-all-done.1 = bf16[32,32,448]{2,1,0:T(8,128)(2,1)S(1)} async-done(((bf16[32,32,448]{2,1,0:T(8,128)(2,1)}), bf16[32,32,448]{2,1,0:T(8,128)(2,1)S(1)}, u32[]{:S(2)}, u32[]{:S(2)}) %all-to-all-start.1) | async-done | bytes 917536 | tf_op jit(solution)/shard_map/all_to_all | solution.py:101
  267.3 8.2 %all-to-all-start.3 = ((bf16[32,32,448]{2,1,0:T(8,128)(2,1)}), bf16[32,32,448]{2,1,0:T(8,128)(2,1)S(1)}, u32[]{:S(2)}, u32[]{:S(2)}) async-start(bf16[32,32,448]{2,1,0:T(8,128)(2,1)} %bitcast.13), calls=%async_computation.3 | async-start | bytes 2097152 | tf_op jit(solution)/shard_map/all_to_all | solution.py:127
  277.3 2.8 collective-permute-start.3
  280.1 30.9 %collective-permute-done.3 = bf16[1024,448]{0,1:T(8,128)(2,1)S(1)} collective-permute-done((bf16[1024,448]{0,1:T(8,128)(2,1)S(1)}, bf16[1024,448]{0,1:T(8,128)(2,1)S(1)}, u32[]{:S(2)}, u32[]{:S(2)}) %collective-permute-start.3) | collective-permute-done | bytes 917536 | tf_op jit(solution)/shard_map/ppermute | solution.py:18
  311.0 6.7 %fusion.18 = (bf16[1,1024,448]{1,2,0:T(8,128)(2,1)}, f32[1,1024,448]{1,2,0:T(8,128)}, f32[1,1024,448]{1,2,0:T(8,128)}) fusion(f32[1,1024,448]{1,2,0:T(8,128)} %param.22, bf16[1024,448]{0,1:T(8,128)(2,1)} %collective-permute-done.2, pred[]{:T(512)S(6)} %gt.21, f32[1,1024,448]{1,2,0:T(8,128)} %param.23, bf16[1024,448]{0,1:T(8,128)(2,1)S(1)} %collective-permute-done.3, ...), kind=kOutput, calls=%fused_computation.42 | convolution fusion | flops 945946624 | bytes 13107201 | tf_op jit(solution)/shard_map/dot_general | solution.py:111
  (44 shorter events, 17.8 us)
Async XLA Ops:
  14.9 4.0 %copy-start.6 = (f32[1,32,32]{2,1,0:T(8,128)S(1)}, f32[1,32,32]{2,1,0:T(8,128)}, u32[]{:S(2)}) copy-start(f32[1,32,32]{2,1,0:T(8,128)} %param.17) | copy-start | bytes 12292
  14.9 4.1 %copy-start.8 = (s32[16]{0:T(128)S(1)}, s32[16]{0:T(128)}, u32[]{:S(2)}) copy-start(s32[16]{0:T(128)} %param.18) | copy-start | bytes 196
  22.4 36.8 %all-to-all-start.2 = ((bf16[32,32,448]{2,1,0:T(8,128)(2,1)}), bf16[32,32,448]{2,1,0:T(8,128)(2,1)S(1)}, u32[]{:S(2)}, u32[]{:S(2)}) async-start(bf16[32,32,448]{2,1,0:T(8,128)(2,1)} %bitcast.11), calls=%async_computation.2 | async-start | bytes 2097152 | tf_op jit(solution)/shard_map/all_to_all | solution.py:108
  35.8 88.4 %collective-permute-start = (bf16[448,2048]{1,0:T(8,128)(2,1)S(1)}, bf16[448,2048]{1,0:T(8,128)(2,1)}, u32[]{:S(2)}, u32[]{:S(2)}) collective-permute-start(bf16[448,2048]{1,0:T(8,128)(2,1)S(1)} %pad_maximum_fusion), channel_id=1, source_target_pairs={{0,16},{16,0},{1,17},{17,1},{2,18},{18,2},{3,19},{19,3},{4,20},{20... | collective-permute-start | bytes 5505032 | tf_op jit(solution)/shard_map/ppermute | solution.py:18
  59.1 65.1 %copy-start.4 = (bf16[32,32,448]{2,1,0:T(8,128)(2,1)}, bf16[32,32,448]{2,1,0:T(8,128)(2,1)S(1)}, u32[]{:S(2)}) copy-start(bf16[32,32,448]{2,1,0:T(8,128)(2,1)S(1)} %all-to-all-done.2) | copy-start | bytes 2752516
  59.1 65.1 %all-to-all-start = ((bf16[32,32,448]{2,1,0:T(8,128)(2,1)}), bf16[32,32,448]{2,1,0:T(8,128)(2,1)}, u32[]{:S(2)}, u32[]{:S(2)}) async-start(bf16[32,32,448]{2,1,0:T(8,128)(2,1)} %bitcast.2), calls=%async_computation | async-start | bytes 2097152 | tf_op jit(solution)/shard_map/all_to_all | solution.py:84
  67.6 153.0 %all-reduce.3.cloned.1.call-start = ((), (), s32[]{:S(2)}) async-start(), calls=%async_computation.4 | async-start | bytes 12582912 | tf_op jit(solution)/shard_map/psum | solution.py:89
  67.6 52.7 %collective-permute-start.1 = (bf16[1024,448]{0,1:T(8,128)(2,1)}, bf16[1024,448]{0,1:T(8,128)(2,1)}, u32[]{:S(2)}, u32[]{:S(2)}) collective-permute-start(bf16[1024,448]{0,1:T(8,128)(2,1)} %bitcast.74), channel_id=1, source_target_pairs={{0,16},{16,0},{1,17},{17,1},{2,18},{18,2},{3,19},{19,3},{4,20},{20... | collective-permute-start | bytes 2752520 | tf_op jit(solution)/shard_map/ppermute | solution.py:18
  220.5 3.4 %copy-start.3 = (bf16[1024,1024]{1,0:T(8,128)(2,1)S(1)}, bf16[1024,1024]{1,0:T(8,128)(2,1)}, u32[]{:S(2)}) copy-start(bf16[1024,1024]{1,0:T(8,128)(2,1)} %get-tuple-element.7) | copy-start | bytes 6291460
  223.9 5.0 %copy-start.7 = (bf16[1,1024,448]{1,2,0:T(8,128)(2,1)S(1)}, bf16[1,1024,448]{1,2,0:T(8,128)(2,1)}, u32[]{:S(2)}) copy-start(bf16[1,1024,448]{1,2,0:T(8,128)(2,1)} %param.21) | copy-start | bytes 2752516
  227.6 1.3 copy-start
  231.4 35.9 %all-to-all-start.1 = ((bf16[32,32,448]{2,1,0:T(8,128)(2,1)}), bf16[32,32,448]{2,1,0:T(8,128)(2,1)S(1)}, u32[]{:S(2)}, u32[]{:S(2)}) async-start(bf16[32,32,448]{2,1,0:T(8,128)(2,1)} %bitcast.7), calls=%async_computation.1 | async-start | bytes 2097152 | tf_op jit(solution)/shard_map/all_to_all | solution.py:101
  242.2 5.5 %copy-start.2 = (bf16[1024,1024]{1,0:T(8,128)(2,1)S(1)}, bf16[1024,1024]{1,0:T(8,128)(2,1)}, u32[]{:S(2)}) copy-start(bf16[1024,1024]{1,0:T(8,128)(2,1)} %get-tuple-element.9) | copy-start | bytes 6291460
  244.9 35.3 %collective-permute-start.2 = (bf16[1024,448]{0,1:T(8,128)(2,1)}, bf16[1024,448]{0,1:T(8,128)(2,1)}, u32[]{:S(2)}, u32[]{:S(2)}) collective-permute-start(bf16[1024,448]{0,1:T(8,128)(2,1)} %bitcast_convert_fusion.1), channel_id=1, source_target_pairs={{0,16},{16,0},{1,17},{17,1},{2,18},{18,2},{3,19},{19,3},{4,20},{20... | collective-permute-start | bytes 2752520 | tf_op jit(solution)/shard_map/ppermute | solution.py:18
  267.3 43.7 %copy-start.5 = (bf16[32,32,448]{2,1,0:T(8,128)(2,1)S(1)}, bf16[32,32,448]{2,1,0:T(8,128)(2,1)}, u32[]{:S(2)}) copy-start(bf16[32,32,448]{2,1,0:T(8,128)(2,1)} %copy-done.4) | copy-start | bytes 2752516
  267.3 50.4 %all-to-all-start.3 = ((bf16[32,32,448]{2,1,0:T(8,128)(2,1)}), bf16[32,32,448]{2,1,0:T(8,128)(2,1)S(1)}, u32[]{:S(2)}, u32[]{:S(2)}) async-start(bf16[32,32,448]{2,1,0:T(8,128)(2,1)} %bitcast.13), calls=%async_computation.3 | async-start | bytes 2097152 | tf_op jit(solution)/shard_map/all_to_all | solution.py:127
  275.5 35.5 %copy-start.1 = (bf16[1024,1024]{1,0:T(8,128)(2,1)S(1)}, bf16[1024,1024]{1,0:T(8,128)(2,1)}, u32[]{:S(2)}) copy-start(bf16[1024,1024]{1,0:T(8,128)(2,1)} %copy-done) | copy-start | bytes 6291460
  277.3 33.7 %collective-permute-start.3 = (bf16[1024,448]{0,1:T(8,128)(2,1)S(1)}, bf16[1024,448]{0,1:T(8,128)(2,1)S(1)}, u32[]{:S(2)}, u32[]{:S(2)}) collective-permute-start(bf16[1024,448]{0,1:T(8,128)(2,1)S(1)} %bitcast_convert_fusion), channel_id=1, source_target_pairs={{0,16},{16,0},{1,17},{17,1},{2,18},{18,2},{3,19},{19,3},{4,20},{20... | collective-permute-start | bytes 2752520 | tf_op jit(solution)/shard_map/ppermute | solution.py:18
Sparse Core Ops, SparseCore 0:
  130.4 90.0 all-reduce.2
where the time goes:
time: 330 us
  waiting for transfers between devices  203 us (62%)
  starting transfers between devices  50.4 us (15%)
  matrix products  26.5 us (8%)
  other arithmetic  18.7 us (6%)
  local copies, waits for them, and re-layouts  15.9 us (5%)
  between operations  14.9 us (5%)
    psum x1, waiting for transfers between devices, shards(): lax.psum(jnp.dot(arrived, gate_up, preferred_element_type=jnp.float32).as...  90.2 us
    ppermute x4, waiting for transfers between devices, partner(): return lax.ppermute(block, axis, route)  79.5 us
    all_to_all x1, waiting for transfers between devices, shards(): lax.all_to_all(to_hosts(grad_slots), 'expert', split_axis=0, concat_axis=...  20.5 us
    all_to_all x1, waiting for transfers between devices, shards(): lax.all_to_all(outputs, 'expert', split_axis=0, concat_axis=0, tiled=True)  12.8 us
    all_to_all x1, starting transfers between devices, shards(): lax.all_to_all(to_hosts(grad_slots), 'expert', split_axis=0, concat_axis=...  11.9 us
    ppermute x4, starting transfers between devices, partner(): return lax.ppermute(block, axis, route)  11.2 us
    all_to_all x1, starting transfers between devices, shards(): lax.all_to_all(outputs, 'expert', split_axis=0, concat_axis=0, tiled=True)  10.7 us
    all_to_all x1, starting transfers between devices, shards(): lax.all_to_all(to_hosts(outgoing), 'expert', split_axis=0, concat_axis=0,...  8.45 us
  transfers between devices with their start and end apart: 9, of which 5 were waited for; matrix products, arithmetic and copies ran while one was open for 7% of the time, Pallas kernels for 0%

commit v1 on v0

--- a/solution.py
+++ b/solution.py
@@ -86,8 +86,11 @@
     ).reshape(-1, model_cols)
     hidden_units = down_proj.shape[0]
     contract_last = (((1,), (1,)), ((), ()))
-    preact = lax.psum(
-        jnp.dot(arrived, gate_up, preferred_element_type=jnp.float32).astype(jnp.bfloat16), "dp"
+    preact = jnp.sum(
+        lax.all_gather(
+            jnp.dot(arrived, gate_up, preferred_element_type=jnp.float32).astype(jnp.bfloat16), "dp"
+        ),
+        axis=0,
     ).astype(jnp.float32)
     gate_pre = preact[:, :hidden_units]
     up_pre = preact[:, hidden_units:]

time: 330 us -> 415 us (1.26); the launches traced: 330 us -> 407 us
  waiting for transfers between devices: 203 us -> 263 us
  other arithmetic: 18.7 us -> 39.6 us
    all_gather x0 -> x1, waiting for transfers between devices: none -> 116 us  [shards(): lax.all_gather(jnp.dot(arrived, gate_up, preferred_element_type=jnp.float...]
    psum x1, waiting for transfers between devices: 90.2 us -> 51.2 us  [shards(): lax.psum(lax.dot_general(arrived_grad, down_proj, contract_last, preferre...]
    all_to_all x1, waiting for transfers between devices: 0.01 us -> 28.9 us  [shards(): lax.all_to_all(to_hosts(outgoing), 'expert', split_axis=0, concat_axis=0,...]
    ppermute x4, waiting for transfers between devices: 79.5 us -> 56 us  [partner(): return lax.ppermute(block, axis, route)]
    all_to_all x1, waiting for transfers between devices: 20.5 us -> 0.01 us  [shards(): lax.all_to_all(to_hosts(grad_slots), 'expert', split_axis=0, concat_axis=...]
    reduce_sum x0 -> x1, other arithmetic: none -> 14.3 us  [shards(): jnp.sum(lax.all_gather(jnp.dot(arrived, gate_up, preferred_element_type=j...]
  transfers between devices with their start and end apart: 9 -> 10, of which waited for: 5 -> 6; matrix products, arithmetic and copies ran while one was open for 7% -> 13% of each run, Pallas kernels for 0% -> 0%
where the time goes in v1:
time: 415 us; the launch traced here: 407 us
  waiting for transfers between devices  263 us (63%)
  starting transfers between devices  51.7 us (12%)
  other arithmetic  39.6 us (10%)
  matrix products  23.6 us (6%)
  between operations  14.9 us (4%)
  local copies, waits for them, and re-layouts  13.4 us (3%)
    all_gather x1, waiting for transfers between devices, shards(): lax.all_gather(jnp.dot(arrived, gate_up, preferred_element_type=jnp.float...  116 us
    ppermute x4, waiting for transfers between devices, partner(): return lax.ppermute(block, axis, route)  56 us
    psum x1, waiting for transfers between devices, shards(): lax.psum(lax.dot_general(arrived_grad, down_proj, contract_last, preferre...  51.2 us
    all_to_all x1, waiting for transfers between devices, shards(): lax.all_to_all(to_hosts(outgoing), 'expert', split_axis=0, concat_axis=0,...  28.9 us
    reduce_sum x1, other arithmetic, shards(): jnp.sum(lax.all_gather(jnp.dot(arrived, gate_up, preferred_element_type=j...  14.3 us
    all_to_all x1, starting transfers between devices, shards(): lax.all_to_all(to_hosts(grad_slots), 'expert', split_axis=0, concat_axis=...  12.7 us
    ppermute x4, starting transfers between devices, partner(): return lax.ppermute(block, axis, route)  12.4 us
    all_to_all x1, waiting for transfers between devices, shards(): lax.all_to_all(outputs, 'expert', split_axis=0, concat_axis=0, tiled=True)  11.2 us
  transfers between devices with their start and end apart: 10, of which 6 were waited for; matrix products, arithmetic and copies ran while one was open for 13% of the time, Pallas kernels for 0%

profile of v1, /device:TPU:1, one launch (start us, length us, event | category | flops | bytes accessed | tf_op | source)
XLA Modules:
  0.0 406.6 jit_solution(8459296728860079441)
XLA Ops:
  7.2 2.9 pad_maximum_fusion
  10.1 3.6 collective-permute-start
  14.3 4.0 gather_fusion
  18.3 4.0 gather_fusion.1
  25.7 9.3 %all-to-all-start = ((bf16[32,32,448]{2,1,0:T(8,128)(2,1)}), bf16[32,32,448]{2,1,0:T(8,128)(2,1)S(1)}, u32[]{:S(2)}, u32[]{:S(2)}) async-start(bf16[32,32,448]{2,1,0:T(8,128)(2,1)} %bitcast.2), calls=%async_computation | async-start | bytes 2097152 | tf_op jit(solution)/shard_map/all_to_all | solution.py:84
  36.3 28.9 %all-to-all-done = bf16[32,32,448]{2,1,0:T(8,128)(2,1)S(1)} async-done(((bf16[32,32,448]{2,1,0:T(8,128)(2,1)}), bf16[32,32,448]{2,1,0:T(8,128)(2,1)S(1)}, u32[]{:S(2)}, u32[]{:S(2)}) %all-to-all-start) | async-done | bytes 917536 | tf_op jit(solution)/shard_map/all_to_all | solution.py:84
  65.3 4.5 %convolution_convert_fusion = bf16[1024,2048]{1,0:T(8,128)(2,1)} fusion(bf16[1024,448]{1,0:T(8,128)(2,1)S(1)} %bitcast.69, bf16[448,2048]{1,0:T(8,128)(2,1)} %collective-permute-done, pred[]{:T(512)S(6)} %gt.21, bf16[448,1024]{1,0:T(8,128)(2,1)S(1)} %bitcast.72, bf16[448,1024]{1,0:T(8,128)(2,1)S(1)} %bitcast.75), kind=kOutput, calls=%fused_computation.15 | convolution fusion | flops 1885732864 | bytes 8781825 | tf_op jit(solution)/shard_map/dot_general | solution.py:91
  69.8 12.7 %all-to-all-start.2 = ((bf16[32,32,448]{2,1,0:T(8,128)(2,1)}), bf16[32,32,448]{2,1,0:T(8,128)(2,1)S(1)}, u32[]{:S(2)}, u32[]{:S(2)}) async-start(bf16[32,32,448]{2,1,0:T(8,128)(2,1)} %bitcast.12), calls=%async_computation.2 | async-start | bytes 2097152 | tf_op jit(solution)/shard_map/all_to_all | solution.py:111
  82.5 3.0 collective-permute-start.1
  85.5 29.8 %collective-permute-done.1 = bf16[1024,448]{0,1:T(8,128)(2,1)S(1)} collective-permute-done((bf16[1024,448]{0,1:T(8,128)(2,1)S(1)}, bf16[1024,448]{0,1:T(8,128)(2,1)S(1)}, u32[]{:S(2)}, u32[]{:S(2)}) %collective-permute-start.1) | collective-permute-done | bytes 917536 | tf_op jit(solution)/shard_map/ppermute | solution.py:18
  118.0 116.0 %all-gather.3.cloned.1.call-done = bf16[8192,2048]{1,0:T(8,128)(2,1)} async-done(((bf16[1024,2048]{1,0:T(8,128)(2,1)}), bf16[8192,2048]{1,0:T(8,128)(2,1)}) %all-gather.3.cloned.1.call-update) | async-done | bytes 33554448 | tf_op jit(solution)/shard_map/all_gather | solution.py:90
  234.0 14.3 %reduce_sum.22 = bf16[1024,2048]{1,0:T(8,128)(2,1)} reduce(bf16[8,1024,2048]{2,1,0:T(8,128)(2,1)} %bitcast.60, bf16[]{:T(256)} %constant.22.clone.1), dimensions={0}, to_apply=%region_1.3 | reduce | flops 14680064 | bytes 37748736 | tf_op jit(solution)/shard_map/reduce_sum | solution.py:89
  248.2 6.5 %convert_element_type.71 = f32[1024,2048]{1,0:T(8,128)} convert(bf16[1024,2048]{1,0:T(8,128)(2,1)} %reduce_sum.22) | non-fusion elementwise | flops 2097152 | bytes 12582912 | tf_op jit(solution)/shard_map/convert_element_type | solution.py:94
  254.8 51.2 %all-reduce.2.cloned.1.call-done = bf16[1024,1024]{1,0:T(8,128)(2,1)} async-done(((bf16[1024,1024]{1,0:T(8,128)(2,1)}), bf16[1024,1024]{1,0:T(8,128)(2,1)}) %all-reduce.2.cloned.1.call-update) | async-done | bytes 2097168 | tf_op jit(solution)/shard_map/psum | solution.py:117
  306.0 6.5 %fusion.2 = (bf16[1024,1024]{1,0:T(8,128)(2,1)S(1)}, bf16[1024,1024]{1,0:T(8,128)(2,1)}, bf16[1024,1024]{1,0:T(8,128)(2,1)S(1)}) fusion(bf16[1024,1024]{1,0:T(8,128)(2,1)} %all-reduce.2.cloned.1.call-done, f32[1024,2048]{1,0:T(8,128)} %convert_element_type.71), kind=kLoop, calls=%fused_computation.6 | loop fusion | flops 17825792 | bytes 16777216 | tf_op jit(solution)/shard_map/convert.1
  316.3 9.5 %all-to-all-start.1 = ((bf16[32,32,448]{2,1,0:T(8,128)(2,1)}), bf16[32,32,448]{2,1,0:T(8,128)(2,1)S(1)}, u32[]{:S(2)}, u32[]{:S(2)}) async-start(bf16[32,32,448]{2,1,0:T(8,128)(2,1)} %bitcast.8), calls=%async_computation.1 | async-start | bytes 2097152 | tf_op jit(solution)/shard_map/all_to_all | solution.py:104
  325.8 2.7 bitcast_convert_fusion.1
  328.5 2.7 collective-permute-start.2
  331.3 4.6 %fusion.13 = bf16[1024,448]{0,1:T(8,128)(2,1)} fusion(bf16[1024,1024]{1,0:T(8,128)(2,1)S(1)} %copy-done.2, bf16[1024,1024]{1,0:T(8,128)(2,1)S(1)} %get-tuple-element.6, bf16[448,2048]{1,0:T(8,128)(2,1)} %collective-permute-done, pred[]{:T(512)S(6)} %gt.21, bf16[448,1024]{1,0:T(8,128)(2,1)} %bitcast.71, bf16[448,1024]{1,0:T(8,128)(2,1)} %bitcast.74), kind=kOutput, calls=%fused_computation.34 | convolution fusion | flops 1892483072 | bytes 8781825 | tf_op jit(solution)/shard_map/dot_general | solution.py:123
  338.1 11.2 %all-to-all-done.1 = bf16[32,32,448]{2,1,0:T(8,128)(2,1)S(1)} async-done(((bf16[32,32,448]{2,1,0:T(8,128)(2,1)}), bf16[32,32,448]{2,1,0:T(8,128)(2,1)S(1)}, u32[]{:S(2)}, u32[]{:S(2)}) %all-to-all-start.1) | async-done | bytes 917536 | tf_op jit(solution)/shard_map/all_to_all | solution.py:104
  349.3 7.8 %all-to-all-start.3 = ((bf16[32,32,448]{2,1,0:T(8,128)(2,1)}), bf16[32,32,448]{2,1,0:T(8,128)(2,1)S(1)}, u32[]{:S(2)}, u32[]{:S(2)}) async-start(bf16[32,32,448]{2,1,0:T(8,128)(2,1)} %bitcast.14), calls=%async_computation.3 | async-start | bytes 2097152 | tf_op jit(solution)/shard_map/all_to_all | solution.py:130
  358.9 3.0 collective-permute-start.3
  361.9 26.2 %collective-permute-done.3 = bf16[1024,448]{0,1:T(8,128)(2,1)S(1)} collective-permute-done((bf16[1024,448]{0,1:T(8,128)(2,1)S(1)}, bf16[1024,448]{0,1:T(8,128)(2,1)S(1)}, u32[]{:S(2)}, u32[]{:S(2)}) %collective-permute-start.3) | collective-permute-done | bytes 917536 | tf_op jit(solution)/shard_map/ppermute | solution.py:18
  388.1 6.7 %fusion.18 = (bf16[1,1024,448]{1,2,0:T(8,128)(2,1)}, f32[1,1024,448]{1,2,0:T(8,128)}, f32[1,1024,448]{1,2,0:T(8,128)}) fusion(f32[1,1024,448]{1,2,0:T(8,128)} %param.22, bf16[1024,448]{0,1:T(8,128)(2,1)} %collective-permute-done.2, pred[]{:T(512)S(6)} %gt.21, f32[1,1024,448]{1,2,0:T(8,128)} %param.23, bf16[1024,448]{0,1:T(8,128)(2,1)S(1)} %collective-permute-done.3, ...), kind=kOutput, calls=%fused_computation.42 | convolution fusion | flops 945946624 | bytes 13107201 | tf_op jit(solution)/shard_map/dot_general | solution.py:114
  (64 shorter events, 20.1 us)
Async XLA Ops:
  7.2 6.5 %copy-start.9 = (s32[1,32,32]{2,1,0:T(8,128)S(1)}, s32[1,32,32]{2,1,0:T(8,128)}, u32[]{:S(2)}) copy-start(s32[1,32,32]{2,1,0:T(8,128)} %param.15) | copy-start | bytes 12292
  7.2 6.6 %copy-start.11 = (s32[1,32]{1,0:T(1,128)S(1)}, s32[1,32]{1,0:T(1,128)}, u32[]{:S(2)}) copy-start(s32[1,32]{1,0:T(1,128)} %param.16) | copy-start | bytes 388
  7.2 6.8 %copy-start.7 = (bf16[256,448]{0,1:T(8,128)(2,1)S(1)}, bf16[256,448]{0,1:T(8,128)(2,1)}, u32[]{:S(2)}) copy-start(bf16[256,448]{0,1:T(8,128)(2,1)} %param.13) | copy-start | bytes 688132
  7.2 6.9 %copy-start.8 = (bf16[256,448]{0,1:T(8,128)(2,1)S(1)}, bf16[256,448]{0,1:T(8,128)(2,1)}, u32[]{:S(2)}) copy-start(bf16[256,448]{0,1:T(8,128)(2,1)} %param.14) | copy-start | bytes 688132
  10.1 55.1 %collective-permute-start = (bf16[448,2048]{1,0:T(8,128)(2,1)}, bf16[448,2048]{1,0:T(8,128)(2,1)}, u32[]{:S(2)}, u32[]{:S(2)}) collective-permute-start(bf16[448,2048]{1,0:T(8,128)(2,1)} %pad_maximum_fusion), channel_id=1, source_target_pairs={{0,16},{16,0},{1,17},{17,1},{2,18},{18,2},{3,19},{19,3},{4,20},{20... | collective-permute-start | bytes 5505032 | tf_op jit(solution)/shard_map/ppermute | solution.py:18
  18.2 4.0 copy-start.10
  18.3 4.1 %copy-start.16 = (s32[16]{0:T(128)S(1)}, s32[16]{0:T(128)}, u32[]{:S(2)}) copy-start(s32[16]{0:T(128)} %param.18) | copy-start | bytes 196
  25.7 39.6 %copy-start.5 = (bf16[1,448,1024]{2,1,0:T(8,128)(2,1)S(1)}, bf16[1,448,1024]{2,1,0:T(8,128)(2,1)}, u32[]{:S(2)}) copy-start(bf16[1,448,1024]{2,1,0:T(8,128)(2,1)} %param.20) | copy-start | bytes 2752516
  25.7 39.6 %copy-start.6 = (bf16[1,448,1024]{2,1,0:T(8,128)(2,1)S(1)}, bf16[1,448,1024]{2,1,0:T(8,128)(2,1)}, u32[]{:S(2)}) copy-start(bf16[1,448,1024]{2,1,0:T(8,128)(2,1)} %param.19) | copy-start | bytes 2752516
  25.7 39.6 %all-to-all-start = ((bf16[32,32,448]{2,1,0:T(8,128)(2,1)}), bf16[32,32,448]{2,1,0:T(8,128)(2,1)S(1)}, u32[]{:S(2)}, u32[]{:S(2)}) async-start(bf16[32,32,448]{2,1,0:T(8,128)(2,1)} %bitcast.2), calls=%async_computation | async-start | bytes 2097152 | tf_op jit(solution)/shard_map/all_to_all | solution.py:84
  35.0 199.0 %all-gather.3.cloned.1.call-start = ((), (), s32[]{:S(2)}) async-start(), calls=%async_computation.5 | async-start | bytes 37748736 | tf_op jit(solution)/shard_map/all_gather | solution.py:90
  69.7 12.7 %copy-start.12 = (bf16[1,1024,448]{1,2,0:T(8,128)(2,1)S(1)}, bf16[1,1024,448]{1,2,0:T(8,128)(2,1)}, u32[]{:S(2)}) copy-start(bf16[1,1024,448]{1,2,0:T(8,128)(2,1)} %param.21) | copy-start | bytes 2752516
  69.8 45.6 %all-to-all-start.2 = ((bf16[32,32,448]{2,1,0:T(8,128)(2,1)}), bf16[32,32,448]{2,1,0:T(8,128)(2,1)S(1)}, u32[]{:S(2)}, u32[]{:S(2)}) async-start(bf16[32,32,448]{2,1,0:T(8,128)(2,1)} %bitcast.12), calls=%async_computation.2 | async-start | bytes 2097152 | tf_op jit(solution)/shard_map/all_to_all | solution.py:111
  82.4 223.5 %all-reduce.2.cloned.1.call-start = ((), (), s32[]{:S(2)}) async-start(), calls=%async_computation.4 | async-start | bytes 4194304 | tf_op jit(solution)/shard_map/psum | solution.py:117
  82.5 32.8 %collective-permute-start.1 = (bf16[1024,448]{0,1:T(8,128)(2,1)S(1)}, bf16[1024,448]{0,1:T(8,128)(2,1)S(1)}, u32[]{:S(2)}, u32[]{:S(2)}) collective-permute-start(bf16[1024,448]{0,1:T(8,128)(2,1)S(1)} %bitcast.77), channel_id=1, source_target_pairs={{0,16},{16,0},{1,17},{17,1},{2,18},{18,2},{3,19},{19,3},{4,20},{20... | collective-permute-start | bytes 2752520 | tf_op jit(solution)/shard_map/ppermute | solution.py:18
  306.0 7.8 %copy-start.13 = (bf16[1,1024,448]{1,2,0:T(8,128)(2,1)S(1)}, bf16[1,1024,448]{1,2,0:T(8,128)(2,1)}, u32[]{:S(2)}) copy-start(bf16[1,1024,448]{1,2,0:T(8,128)(2,1)} %param.21) | copy-start | bytes 2752516
  306.0 7.8 %copy-start.15 = (bf16[1024,448]{0,1:T(8,128)(2,1)S(1)}, bf16[1024,448]{0,1:T(8,128)(2,1)}, u32[]{:S(2)}) copy-start(bf16[1024,448]{0,1:T(8,128)(2,1)} %copy-done.14) | copy-start | bytes 2752516
  316.3 33.1 %all-to-all-start.1 = ((bf16[32,32,448]{2,1,0:T(8,128)(2,1)}), bf16[32,32,448]{2,1,0:T(8,128)(2,1)S(1)}, u32[]{:S(2)}, u32[]{:S(2)}) async-start(bf16[32,32,448]{2,1,0:T(8,128)(2,1)} %bitcast.8), calls=%async_computation.1 | async-start | bytes 2097152 | tf_op jit(solution)/shard_map/all_to_all | solution.py:104
  325.8 5.5 %copy-start.2 = (bf16[1024,1024]{1,0:T(8,128)(2,1)S(1)}, bf16[1024,1024]{1,0:T(8,128)(2,1)}, u32[]{:S(2)}) copy-start(bf16[1024,1024]{1,0:T(8,128)(2,1)} %get-tuple-element.7) | copy-start | bytes 6291460
  328.5 33.4 %collective-permute-start.2 = (bf16[1024,448]{0,1:T(8,128)(2,1)}, bf16[1024,448]{0,1:T(8,128)(2,1)}, u32[]{:S(2)}, u32[]{:S(2)}) collective-permute-start(bf16[1024,448]{0,1:T(8,128)(2,1)} %bitcast_convert_fusion.1), channel_id=1, source_target_pairs={{0,16},{16,0},{1,17},{17,1},{2,18},{18,2},{3,19},{19,3},{4,20},{20... | collective-permute-start | bytes 2752520 | tf_op jit(solution)/shard_map/ppermute | solution.py:18
  349.3 38.8 %copy-start.4 = (bf16[32,32,448]{2,1,0:T(8,128)(2,1)S(1)}, bf16[32,32,448]{2,1,0:T(8,128)(2,1)}, u32[]{:S(2)}) copy-start(bf16[32,32,448]{2,1,0:T(8,128)(2,1)} %copy-done.3) | copy-start | bytes 2752516
  349.3 45.5 %all-to-all-start.3 = ((bf16[32,32,448]{2,1,0:T(8,128)(2,1)}), bf16[32,32,448]{2,1,0:T(8,128)(2,1)S(1)}, u32[]{:S(2)}, u32[]{:S(2)}) async-start(bf16[32,32,448]{2,1,0:T(8,128)(2,1)} %bitcast.14), calls=%async_computation.3 | async-start | bytes 2097152 | tf_op jit(solution)/shard_map/all_to_all | solution.py:130
  357.1 31.0 %copy-start.1 = (bf16[1024,1024]{1,0:T(8,128)(2,1)S(1)}, bf16[1024,1024]{1,0:T(8,128)(2,1)}, u32[]{:S(2)}) copy-start(bf16[1024,1024]{1,0:T(8,128)(2,1)} %copy-done) | copy-start | bytes 6291460
  358.9 29.2 %collective-permute-start.3 = (bf16[1024,448]{0,1:T(8,128)(2,1)S(1)}, bf16[1024,448]{0,1:T(8,128)(2,1)S(1)}, u32[]{:S(2)}, u32[]{:S(2)}) collective-permute-start(bf16[1024,448]{0,1:T(8,128)(2,1)S(1)} %bitcast_convert_fusion), channel_id=1, source_target_pairs={{0,16},{16,0},{1,17},{17,1},{2,18},{18,2},{3,19},{19,3},{4,20},{20... | collective-permute-start | bytes 2752520 | tf_op jit(solution)/shard_map/ppermute | solution.py:18
  (3 other events, 6.6 us)
Sparse Core Ops, SparseCore 0:
  69.9 164.0 all-gather.2
  236.3 69.5 all-reduce.1
